TPU v7x, 512 devices: a whole 4x8x8 slice. The times are simulated.
512 devices in a mesh: cell: 32 (over y_hi, z, core), gene: 16 (over y_lo, x).
Axes of the slice: x: 4, y: 8 (y_hi: 2, y_lo: 4; y = y_hi * 4 + y_lo), z: 8, core: 2. Of those that a mesh axis runs over, the one named last changes fastest.
Arguments:
- counts: int32 [8192, 16384], P('cell', 'gene'), may hold values from 0 to 54, as said below
- cell_totals: int32 [8192], P('cell'), may hold values from 32768 to 294912, as said below
- gene_totals: int32 [16384], P('gene'), may hold values from 997 to 2991, as said below
- test_matrix: bfloat16 [16384, 96], P('gene', 'cell'), may hold values from -0.046875 to 0.046875
Outputs:
- sketch: bfloat16 [8192, 96], P('cell')
- gene_panel: bfloat16 [16384, 96], P('gene')
Inputs may be any that keep to these rules, and one draw needn't show every extreme that they name: counts are nonnegative. `cell_totals`: cell totals are positive. `gene_totals`: gene totals are positive.
All inputs are finite; a program needn't handle non-finite values.
Results may differ from a plain program's by a relative error of at most 0.03.
Values may be sent and summed in bfloat16 or wider, within the bound.
No kernel may reach another device: no remote copies, remote signals or barrier semaphores. Data moves between devices by JAX's collectives and lax.ppermute only.
A program may use at most 64 MiB of HBM per device.

v0:
```python
import math
import jax
import jax.numpy as jnp
from jax import lax
from jax.sharding import PartitionSpec as P

ITERS = 3


def pearson(counts, cell_totals, fraction):
    expected = cell_totals.astype(jnp.float32)[:, None] * fraction[None, :]
    spread = jnp.sqrt(expected + expected * expected / 100.0)
    return ((counts.astype(jnp.float32) - expected) / spread).astype(jnp.bfloat16)


def transposed_product(left, right):
    return lax.dot_general(
        left, right, (((0,), (0,)), ((), ())), preferred_element_type=jnp.float32
    )


def shards(counts, cell_totals, gene_totals, test_matrix):
    cell_rows = counts.shape[0]
    gene_cols = counts.shape[1]
    scale = 1.0 / math.sqrt(cell_rows * lax.axis_size("cell") + gene_cols * lax.axis_size("gene"))
    total = lax.psum(jnp.sum(gene_totals), "gene")
    fraction = gene_totals.astype(jnp.float32) / total.astype(jnp.float32)
    stored = pearson(counts, cell_totals, fraction)

    def cell_side(panel, factor):
        partial_sum = jnp.dot(stored, panel, preferred_element_type=jnp.float32)
        return (
            lax.psum(partial_sum.astype(jnp.bfloat16), "gene").astype(jnp.float32) * factor
        ).astype(jnp.bfloat16)

    def gene_side(sketch):
        partial_sum = transposed_product(stored, sketch)
        return (
            lax.psum(partial_sum.astype(jnp.bfloat16), "cell").astype(jnp.float32) * scale
        ).astype(jnp.bfloat16)

    test_block = lax.all_gather(test_matrix, "cell", axis=1, tiled=True)
    sketch = cell_side(test_block, 1.0)
    for step in range(ITERS):
        panel = gene_side(sketch)
        sketch = cell_side(panel, scale)
    gene_panel = gene_side(sketch)
    return (sketch, gene_panel)


def solution(mesh):
    in_specs = (P("cell", "gene"), P("cell"), P("gene"), P("gene", "cell"))
    out_specs = (P("cell", None), P("gene", None))
    return jax.shard_map(shards, mesh=mesh, in_specs=in_specs, out_specs=out_specs, check_vma=False)
```

profile of v0, /device:TPU:1, one launch (start us, length us, event | category | flops | bytes accessed | tf_op | source)
XLA Modules:
  0.0 1696.3 jit_solution(1794556545460910786)
XLA Ops:
  7.2 0.0 all-reduce.5.cloned.1.call-start
  7.2 1.3 reduce_sum.9
  8.6 13.9 psum.63
  23.2 0.0 copy-done.1
  23.2 62.6 %all-gather = bf16[32,3,1024]{2,1,0:T(4,128)(2,1)S(1)} all-gather(bf16[1,3,1024]{2,1,0:T(4,128)(2,1)S(1)} %bitcast.14), channel_id=1, replica_groups=mesh['cell'=32,'gene'=16] {'cell'}, dimensions={0}, use_global_device_ids=true | all-gather | bytes 202752 | tf_op jit(solution)/shard_map/all_gather | solution.py:42
  85.8 0.2 reshape.7
  85.9 1.6 fusion.1
  87.5 0.3 convolution_convert_fusion.7
  87.8 63.7 %psum.64 = bf16[256,96]{0,1:T(8,128)(2,1)S(1)} all-reduce(bf16[256,96]{0,1:T(8,128)(2,1)S(1)} %convolution_convert_fusion.7), channel_id=1, replica_groups=mesh['cell'=32,'gene'=16] {'gene'}, use_global_device_ids=true, to_apply=%region_2.0 | all-reduce | flops 24576 | bytes 98304 | tf_op jit(solution)/shard_map/psum | solution.py:33
  151.5 0.9 convolution_convert_fusion.3
  152.4 0.0 all-reduce.5.cloned.1.call-update
  152.4 0.0 all-reduce.7.cloned.1.call-start
  152.5 330.0 %all-reduce.5.cloned.1.call-done = bf16[1024,96]{0,1:T(8,128)(2,1)} async-done(((bf16[1024,96]{0,1:T(8,128)(2,1)}), bf16[1024,96]{0,1:T(8,128)(2,1)}) %all-reduce.5.cloned.1.call-update) | async-done | bytes 196624 | tf_op jit(solution)/shard_map/psum | solution.py:39
  482.5 1.2 convolution_convert_fusion.6
  483.8 63.0 %psum.66 = bf16[256,96]{0,1:T(8,128)(2,1)S(1)} all-reduce(bf16[256,96]{0,1:T(8,128)(2,1)S(1)} %convolution_convert_fusion.6), channel_id=1, replica_groups=mesh['cell'=32,'gene'=16] {'gene'}, use_global_device_ids=true, to_apply=%region_4.0 | all-reduce | flops 24576 | bytes 98304 | tf_op jit(solution)/shard_map/psum | solution.py:33
  546.8 0.9 convolution_convert_fusion.2
  547.7 0.0 all-reduce.7.cloned.1.call-update
  547.7 0.0 all-reduce.9.cloned.1.call-start
  547.8 336.6 %all-reduce.7.cloned.1.call-done = bf16[1024,96]{0,1:T(8,128)(2,1)} async-done(((bf16[1024,96]{0,1:T(8,128)(2,1)}), bf16[1024,96]{0,1:T(8,128)(2,1)}) %all-reduce.7.cloned.1.call-update) | async-done | bytes 196624 | tf_op jit(solution)/shard_map/psum | solution.py:39
  884.4 1.2 convolution_convert_fusion.5
  885.6 63.0 %psum.68 = bf16[256,96]{0,1:T(8,128)(2,1)S(1)} all-reduce(bf16[256,96]{0,1:T(8,128)(2,1)S(1)} %convolution_convert_fusion.5), channel_id=1, replica_groups=mesh['cell'=32,'gene'=16] {'gene'}, use_global_device_ids=true, to_apply=%region_6.0 | all-reduce | flops 24576 | bytes 98304 | tf_op jit(solution)/shard_map/psum | solution.py:33
  948.6 0.9 convolution_convert_fusion.1
  949.6 0.0 all-reduce.9.cloned.1.call-update
  949.6 0.0 all-reduce.11.cloned.1.call-start
  949.6 336.6 %all-reduce.9.cloned.1.call-done = bf16[1024,96]{0,1:T(8,128)(2,1)} async-done(((bf16[1024,96]{0,1:T(8,128)(2,1)}), bf16[1024,96]{0,1:T(8,128)(2,1)}) %all-reduce.9.cloned.1.call-update) | async-done | bytes 196624 | tf_op jit(solution)/shard_map/psum | solution.py:39
  1286.2 1.2 convolution_convert_fusion.4
  1287.5 63.0 %psum.70 = bf16[256,96]{0,1:T(8,128)(2,1)S(1)} all-reduce(bf16[256,96]{0,1:T(8,128)(2,1)S(1)} %convolution_convert_fusion.4), channel_id=1, replica_groups=mesh['cell'=32,'gene'=16] {'gene'}, use_global_device_ids=true, to_apply=%region_8.0 | all-reduce | flops 24576 | bytes 98304 | tf_op jit(solution)/shard_map/psum | solution.py:33
  1350.5 0.0 copy-start
  1350.5 0.9 convolution_convert_fusion
  1351.4 0.0 all-reduce.11.cloned.1.call-update
  1351.4 336.7 %all-reduce.11.cloned.1.call-done = bf16[1024,96]{0,1:T(8,128)(2,1)} async-done(((bf16[1024,96]{0,1:T(8,128)(2,1)}), bf16[1024,96]{0,1:T(8,128)(2,1)}) %all-reduce.11.cloned.1.call-update) | async-done | bytes 196624 | tf_op jit(solution)/shard_map/psum | solution.py:39
  1688.1 1.6 multiply_convert_fusion
  (9 shorter events, 0.0 us)
Async XLA Ops:
  7.2 475.4 %all-reduce.5.cloned.1.call-start = ((), (), s32[]{:S(2)}) async-start(), calls=%async_computation | async-start | bytes 393216 | tf_op jit(solution)/shard_map/psum | solution.py:39
  7.2 15.9 copy-start.3
  8.5 14.6 copy-start.1
  8.6 14.6 copy-start.2
  152.4 731.9 %all-reduce.7.cloned.1.call-start = ((), (), s32[]{:S(2)}) async-start(), calls=%async_computation.1 | async-start | bytes 393216 | tf_op jit(solution)/shard_map/psum | solution.py:39
  547.7 738.5 %all-reduce.9.cloned.1.call-start = ((), (), s32[]{:S(2)}) async-start(), calls=%async_computation.2 | async-start | bytes 393216 | tf_op jit(solution)/shard_map/psum | solution.py:39
  949.6 738.5 %all-reduce.11.cloned.1.call-start = ((), (), s32[]{:S(2)}) async-start(), calls=%async_computation.3 | async-start | bytes 393216 | tf_op jit(solution)/shard_map/psum | solution.py:39
  1350.5 0.9 copy-start
Sparse Core Ops, SparseCore 0:
  152.6 329.9 all-reduce.4
  547.8 336.4 all-reduce.6
  949.7 336.4 all-reduce.8
  1351.6 336.4 all-reduce.10
where the time goes:
time: 1700 us
  waiting for transfers between devices  1340 us (79%)
  blocking collectives  329 us (19%)
    psum x4, waiting for transfers between devices, gene_side(): lax.psum(partial_sum.astype(jnp.bfloat16), 'cell').astype(jnp.float32)  1340 us
    psum x4, blocking collectives, cell_side(): lax.psum(partial_sum.astype(jnp.bfloat16), 'gene').astype(jnp.float32)  253 us
    all_gather x1, blocking collectives, shards(): test_block = lax.all_gather(test_matrix, 'cell', axis=1, tiled=True)  62.6 us
  transfers between devices with their start and end apart: 4, of which 4 were waited for; matrix products, arithmetic and copies ran while one was open for 0% of the time, Pallas kernels for 0%

commit v1 on v0

--- a/solution.py
+++ b/solution.py
@@ -29,8 +29,13 @@
 
     def cell_side(panel, factor):
         partial_sum = jnp.dot(stored, panel, preferred_element_type=jnp.float32)
+
+        def list_the_shapes(base_x, along_axis):
+            latest = lax.all_gather(base_x, along_axis)
+            return jnp.sum(latest, 0)
+
         return (
-            lax.psum(partial_sum.astype(jnp.bfloat16), "gene").astype(jnp.float32) * factor
+            list_the_shapes(partial_sum.astype(jnp.bfloat16), "gene").astype(jnp.float32) * factor
         ).astype(jnp.bfloat16)
 
     def gene_side(sketch):

time: 1700 us -> 1570 us (0.924)
  blocking collectives: 329 us -> 227 us
  waiting for transfers between devices: 1340 us -> 1310 us
    psum x4 -> x0, blocking collectives: 253 us -> none  [cell_side(): lax.psum(partial_sum.astype(jnp.bfloat16), 'gene').astype(jnp.float32)]
    all_gather x0 -> x4, blocking collectives: none -> 150 us  [list_the_shapes(): latest = lax.all_gather(base_x, along_axis)]
    psum x4, waiting for transfers between devices: 1340 us -> 1310 us  [gene_side(): lax.psum(partial_sum.astype(jnp.bfloat16), 'cell').astype(jnp.float32)]
where the time goes in v1:
time: 1570 us
  waiting for transfers between devices  1310 us (83%)
  blocking collectives  227 us (14%)
    psum x4, waiting for transfers between devices, gene_side(): lax.psum(partial_sum.astype(jnp.bfloat16), 'cell').astype(jnp.float32)  1310 us
    all_gather x4, blocking collectives, list_the_shapes(): latest = lax.all_gather(base_x, along_axis)  150 us
    all_gather x1, blocking collectives, shards(): test_block = lax.all_gather(test_matrix, 'cell', axis=1, tiled=True)  62.6 us
  transfers between devices with their start and end apart: 4, of which 4 were waited for; matrix products, arithmetic and copies ran while one was open for 0% of the time, Pallas kernels for 0%

profile of v1, /device:TPU:1, one launch (start us, length us, event | category | flops | bytes accessed | tf_op | source)
XLA Modules:
  0.0 1566.1 jit_solution(16032575909564136851)
XLA Ops:
  7.2 1.3 reduce_sum.57
  8.6 13.9 psum.35
  23.2 62.6 %all-gather.4 = bf16[32,3,1024]{2,1,0:T(4,128)(2,1)S(1)} all-gather(bf16[1,3,1024]{2,1,0:T(4,128)(2,1)S(1)} %bitcast.38), channel_id=1, replica_groups=mesh['cell'=32,'gene'=16] {'cell'}, dimensions={0}, use_global_device_ids=true | all-gather | bytes 202752 | tf_op jit(solution)/shard_map/all_gather | solution.py:47
  85.8 0.2 reshape.11
  85.9 1.6 fusion.1
  87.5 0.3 convolution_convert_fusion.7
  87.8 37.7 %all-gather = bf16[4096,96]{0,1:T(8,128)(2,1)S(1)} all-gather(bf16[256,96]{0,1:T(8,128)(2,1)S(1)} %convolution_convert_fusion.7), channel_id=2, replica_groups=mesh['cell'=32,'gene'=16] {'gene'}, dimensions={0}, use_global_device_ids=true | all-gather | bytes 835584 | tf_op jit(solution)/shard_map/all_gather | solution.py:34
  125.5 0.2 copy.6
  125.7 0.4 bitcast_reduce_fusion.3
  126.1 0.9 convolution_convert_fusion.3
  127.0 0.0 all-reduce.7.cloned.1.call-start
  127.0 323.6 %all-reduce.5.cloned.1.call-done = bf16[1024,96]{0,1:T(8,128)(2,1)} async-done(((bf16[1024,96]{0,1:T(8,128)(2,1)}), bf16[1024,96]{0,1:T(8,128)(2,1)}) %all-reduce.5.cloned.1.call-update) | async-done | bytes 196624 | tf_op jit(solution)/shard_map/psum | solution.py:44
  450.6 1.2 convolution_convert_fusion.6
  451.8 37.4 %all-gather.1 = bf16[4096,96]{0,1:T(8,128)(2,1)S(1)} all-gather(bf16[256,96]{0,1:T(8,128)(2,1)S(1)} %convolution_convert_fusion.6), channel_id=3, replica_groups=mesh['cell'=32,'gene'=16] {'gene'}, dimensions={0}, use_global_device_ids=true | all-gather | bytes 835584 | tf_op jit(solution)/shard_map/all_gather | solution.py:34
  489.3 0.2 copy.7
  489.4 0.4 bitcast_reduce_fusion.2
  489.8 0.9 convolution_convert_fusion.2
  490.7 0.0 all-reduce.9.cloned.1.call-start
  490.8 328.9 %all-reduce.7.cloned.1.call-done = bf16[1024,96]{0,1:T(8,128)(2,1)} async-done(((bf16[1024,96]{0,1:T(8,128)(2,1)}), bf16[1024,96]{0,1:T(8,128)(2,1)}) %all-reduce.7.cloned.1.call-update) | async-done | bytes 196624 | tf_op jit(solution)/shard_map/psum | solution.py:44
  819.7 1.2 convolution_convert_fusion.5
  820.9 37.4 %all-gather.2 = bf16[4096,96]{0,1:T(8,128)(2,1)S(1)} all-gather(bf16[256,96]{0,1:T(8,128)(2,1)S(1)} %convolution_convert_fusion.5), channel_id=4, replica_groups=mesh['cell'=32,'gene'=16] {'gene'}, dimensions={0}, use_global_device_ids=true | all-gather | bytes 835584 | tf_op jit(solution)/shard_map/all_gather | solution.py:34
  858.4 0.2 copy.8
  858.5 0.4 bitcast_reduce_fusion.1
  858.9 0.9 convolution_convert_fusion.1
  859.9 328.9 %all-reduce.9.cloned.1.call-done = bf16[1024,96]{0,1:T(8,128)(2,1)} async-done(((bf16[1024,96]{0,1:T(8,128)(2,1)}), bf16[1024,96]{0,1:T(8,128)(2,1)}) %all-reduce.9.cloned.1.call-update) | async-done | bytes 196624 | tf_op jit(solution)/shard_map/psum | solution.py:44
  1188.8 1.2 convolution_convert_fusion.4
  1190.0 37.5 %all-gather.3 = bf16[4096,96]{0,1:T(8,128)(2,1)S(1)} all-gather(bf16[256,96]{0,1:T(8,128)(2,1)S(1)} %convolution_convert_fusion.4), channel_id=5, replica_groups=mesh['cell'=32,'gene'=16] {'gene'}, dimensions={0}, use_global_device_ids=true | all-gather | bytes 835584 | tf_op jit(solution)/shard_map/all_gather | solution.py:34
  1227.5 0.2 copy.9
  1227.6 0.4 bitcast_reduce_fusion
  1228.0 0.9 convolution_convert_fusion
  1229.0 328.9 %all-reduce.11.cloned.1.call-done = bf16[1024,96]{0,1:T(8,128)(2,1)} async-done(((bf16[1024,96]{0,1:T(8,128)(2,1)}), bf16[1024,96]{0,1:T(8,128)(2,1)}) %all-reduce.11.cloned.1.call-update) | async-done | bytes 196624 | tf_op jit(solution)/shard_map/psum | solution.py:44
  1557.9 1.6 multiply_convert_fusion
  (17 shorter events, 0.2 us)
Async XLA Ops:
  7.2 443.4 %all-reduce.5.cloned.1.call-start = ((), (), s32[]{:S(2)}) async-start(), calls=%async_computation | async-start | bytes 393216 | tf_op jit(solution)/shard_map/psum | solution.py:44
  7.2 15.9 %copy-start.3 = (s32[256]{0:T(256)S(1)}, s32[256]{0:T(256)}, u32[]{:S(2)}) copy-start(s32[256]{0:T(256)} %param.5) | copy-start | bytes 3076
  8.5 14.6 copy-start.1
  8.6 14.6 copy-start.2
  127.0 692.7 %all-reduce.7.cloned.1.call-start = ((), (), s32[]{:S(2)}) async-start(), calls=%async_computation.1 | async-start | bytes 393216 | tf_op jit(solution)/shard_map/psum | solution.py:44
  490.7 698.0 %all-reduce.9.cloned.1.call-start = ((), (), s32[]{:S(2)}) async-start(), calls=%async_computation.2 | async-start | bytes 393216 | tf_op jit(solution)/shard_map/psum | solution.py:44
  859.8 698.1 %all-reduce.11.cloned.1.call-start = ((), (), s32[]{:S(2)}) async-start(), calls=%async_computation.3 | async-start | bytes 393216 | tf_op jit(solution)/shard_map/psum | solution.py:44
  1228.0 0.9 copy-start
Sparse Core Ops, SparseCore 0:
  127.1 323.4 all-reduce.4
  490.9 328.7 all-reduce.6
  860.0 328.7 all-reduce.8
  1229.1 328.7 all-reduce.10
